TPU v7x, 32 devices: a whole 2x2x4 slice. The times are simulated.
32 devices in a mesh: alpha: 16 (over z, y, x), beta: 2 (over core).
Axes of the slice: x: 2, y: 2, z: 4, core: 2. Of those that a mesh axis runs over, the one named last changes fastest.
Arguments:
- coeffs: bfloat16 [1, 2048, 4096], P(None, 'alpha', 'beta'), may hold values from -6 to 6
- beta_list: int32 [32, 8], P('beta'), may hold values from 0 to 31
- beta_kind: int32 [32, 8], P('beta'), may hold values from 0 to 7
- opp_beta_kind: int32 [32, 8], P('beta'), may hold values from 0 to 7
- alpha_list: int32 [16, 4], replicated, may hold values from 0 to 15, as said below
- alpha_kind: int32 [16, 4], replicated, may hold values from 0 to 7
- opp_list: int32 [16, 3], replicated, may hold values from 0 to 15, as said below
- opp_kind: int32 [16, 3], replicated, may hold values from 0 to 7
- beta_table: bfloat16 [8, 128, 128], replicated, may hold values from -0.1875 to 0.1875
- alpha_table: bfloat16 [8, 128, 128], replicated, may hold values from -0.25 to 0.25
- opp_alpha_table: bfloat16 [8, 128, 128], replicated, may hold values from -0.3125 to 0.3125
- opp_beta_table: bfloat16 [8, 128, 128], replicated, may hold values from -0.1875 to 0.1875
Outputs:
- sigma_out: bfloat16 [1, 2048, 4096], P(None, 'alpha', 'beta')
Inputs may be any that keep to these rules, and one draw needn't show every extreme that they name: `alpha_list`: each entry of row i lies within 3 of i; the entries of a row are distinct. `opp_list`: each entry of row i lies within 3 of i; the entries of a row are distinct.
All inputs are finite; a program needn't handle non-finite values.
Results may differ from a plain program's by a relative error of at most 0.0034.
Values may be sent and summed in bfloat16 or wider, within the bound.
A program may use at most 128 MiB of HBM per device.

v0:
```python
import functools

import jax
import jax.numpy as jnp
from jax import lax
from jax.experimental import pallas as pl
from jax.experimental.pallas import tpu as pltpu
from jax.sharding import PartitionSpec as P

GROUP = 4
AHEAD = 6
FORWARD, STRIDE = 12, 10
DELAY = 3
SHIFT = 1.5
BF16, F32 = jnp.bfloat16, jnp.float32
LOW, HIGH, DIAG = range(3)


def picked_tile(block, lists, kinds, table, source):
    kind, found = jnp.int32(0), jnp.int32(0)
    for link in range(lists.shape[0]):
        hit = (lists[link, block] == source).astype(jnp.int32)
        kind += hit * kinds[link, block]
        found += hit
    return table[kind].astype(F32) * found.astype(F32)


def order_of(summed, relayed):
    spread = [(2 * g + 1, summed, "s", g) for g in range(summed // 2)]
    spread += [(2 * g + SHIFT, relayed, "r", g) for g in range(relayed // 2)]
    return [(kind, g) for _, _, kind, g in sorted(spread, key=lambda one: one[0] / one[1])]


def make_plans(summed, relayed):
    wanted = {LOW: [], HIGH: []}
    for kind, g in order_of(summed, relayed):
        first = 2 * g + (summed if kind == "r" else 0)
        wanted[LOW] += [first, first + 1]
        wanted[HIGH] += [first + 1, first]
    late = [c for c in wanted[HIGH] if c >= summed and c % 2 == 0]
    own = {LOW: list(wanted[LOW]), HIGH: [c for c in wanted[HIGH] if c not in late] + late}
    relays = {LOW: [c for c in wanted[HIGH] if c % 2 == 1], HIGH: [c for c in wanted[LOW] if c % 2 == 0]}
    plans, own_at, forward_at = ([], []), ({}, {}), []
    passed = hopped = n = 0
    while own[LOW] or own[HIGH] or relays[LOW] or relays[HIGH] or hopped < relayed:
        for link in (LOW, HIGH):
            other = HIGH if link == LOW else LOW
            due = passed < relayed and n >= FORWARD + STRIDE * passed // 4
            ready = relays[link] and own_at[other].get(relays[link][0], n) + AHEAD <= n
            spare = not own[link] or own[link][0] in late
            if ready:
                plans[link].append(("r", relays[link].pop(0)))
            elif link == HIGH and passed < relayed and (due or spare):
                plans[link].append(("f", summed + passed))
                forward_at.append(n)
                passed += 1
            elif own[link]:
                own_at[link][own[link][0]] = n
                plans[link].append(("o", own[link].pop(0)))
            elif link == LOW and hopped < passed and forward_at[hopped] + AHEAD <= n:
                plans[link].append(("h", summed + hopped))
                hopped += 1
            else:
                plans[link].append((None, None))
        n += 1
    return plans


def slots_of(plans):
    slots, most = ([], []), 0
    for link, plan in enumerate(plans):
        held = []
        for n, (kind, _) in enumerate(plan):
            sure = [k for k in range(n - AHEAD + 1) if plan[k][0] in ("o", "r")]
            free = sure[-1] - AHEAD if sure else -1
            if kind in ("o", "r", "f"):
                spot = next((k for k, user in enumerate(held) if user <= free), len(held))
                held[spot : spot + 1] = [n]
                slots[link].append(spot)
            else:
                slots[link].append(None)
        most = max(most, len(held))
    return slots, most


def closing(plans, summed, relayed):
    at = [{item: n for n, item in enumerate(plan)} for plan in plans]
    last = len(plans[LOW]) - 1
    free, ends = 0, []
    events = [(n, c) for (kind, c), n in at[LOW].items() if kind == "o" and c >= summed]
    for g in range(summed // 2):
        events.append((max(at[LOW]["r", 2 * g + 1], at[HIGH]["r", 2 * g]), 2 * g))
    for n, c in sorted(events):
        free = max(free, n) + (1 if c >= summed else 4)
        if c < summed:
            ends.append((free + DELAY, c // 2))
    for g in range(summed // 2, (summed + relayed) // 2):
        ends.append((max(n for link in (LOW, HIGH) for (_, c), n in at[link].items() if c in (2 * g, 2 * g + 1)), g))
    return [(min(n, last), g) for n, g in sorted(ends)]


def kernel(
    group_count,
    beta_list_hbm,
    beta_kind_hbm,
    opp_beta_kind_hbm,
    alpha_list_hbm,
    alpha_kind_hbm,
    opp_list_hbm,
    opp_kind_hbm,
    coeffs_hbm,
    beta_table_hbm,
    alpha_table_hbm,
    opp_alpha_table_hbm,
    opp_beta_table_hbm,
    out,
    beta_list,
    beta_kind,
    opp_beta_kind,
    alpha_list,
    alpha_kind,
    opp_list,
    opp_kind,
    coeffs,
    tables,
    plane,
    cross,
    sums,
    staged,
    passing,
    whole,
    half,
    acc,
    mine,
    tiles,
    onward,
    load_sem,
    own_send,
    plane_recv,
    relay_send,
    z_send,
    cross_recv,
    sum_send,
    pass_send,
    pass_recv,
    forward_send,
    hop_send,
    pair_send,
    pair_recv,
    half_send,
    half_recv,
):
    rows, cols = coeffs.shape
    kinds, tile = tables.shape[1:3]
    count = cols // tile
    relayed = count // 2
    summed = count - relayed
    plans = make_plans(summed, relayed)
    slots, _ = slots_of(plans)
    beta_table, alpha_table, opp_alpha_table, opp_beta_table = (tables.at[k] for k in range(4))
    me, core = lax.axis_index("alpha"), lax.axis_index("beta")
    z, p = me // GROUP, me % GROUP
    x, y = p % 2, p // 2
    places = (p + 1 - 2 * x, p + 2 - 4 * y, 3 - p)
    mates = tuple(z * GROUP + q for q in places)
    steps = (1 - 2 * x, 1 - 2 * y, 1 - 2 * y)
    middle = x + y == 1
    corner = jnp.logical_not(middle)

    def inside(group):
        return (group >= 0) & (group < group_count)

    has_out = [inside(z + step) for step in steps]
    has_in = [inside(z - step) for step in steps]

    def chip(index):
        return (index, core)

    pair = (me, 1 - core)

    def send(src, dst, send_sem, recv_sem, device):
        return pltpu.make_async_remote_copy(
            src_ref=src,
            dst_ref=dst,
            send_sem=send_sem,
            recv_sem=recv_sem,
            device_id=device,
            device_id_type=pl.DeviceIdType.MESH,
        )

    def sent(ref, sem):
        send(ref, ref, sem, sem, pair).wait_send()

    def arrived(ref, sem):
        send(ref, ref, sem, sem, pair).wait_recv()

    def columns(c):
        return pl.ds(c * tile, tile)

    def wide(g):
        return pl.ds(g * 2 * tile, 2 * tile)

    def both(g):
        return pl.ds(2 * g, 2)

    def own_copy(to, n, c):
        return send(
            coeffs.at[:, columns(c)],
            plane.at[to, c],
            own_send.at[to],
            plane_recv.at[to, slots[to][n]],
            chip(mates[to]),
        )

    def relay_copy(to, n, c):
        return send(
            plane.at[HIGH if to == LOW else LOW, c],
            plane.at[DIAG, c],
            relay_send,
            plane_recv.at[to, slots[to][n]],
            chip(mates[to]),
        )

    def z_copy(r, c):
        return send(
            plane.at[r, c],
            cross.at[r, c],
            z_send.at[r],
            cross_recv.at[min(r, 1), c // 2],
            chip(me + GROUP * steps[r]),
        )

    def sum_copy(c):
        return send(staged.at[c], sums.at[c], sum_send, cross_recv.at[0, c // 2], chip(me + GROUP * steps[LOW]))

    def pass_copy(c):
        k = c - summed
        return send(
            coeffs.at[:, columns(c)], passing.at[k], pass_send, pass_recv.at[k // 2], chip(me - GROUP * steps[HIGH])
        )

    def forward_copy(n, c):
        return send(
            passing.at[c - summed],
            cross.at[HIGH, c],
            forward_send,
            plane_recv.at[HIGH, slots[HIGH][n]],
            chip(mates[HIGH]),
        )

    def hop_copy(c):
        return send(cross.at[HIGH, c], cross.at[DIAG, c], hop_send, cross_recv.at[1, c // 2], chip(mates[LOW]))

    def half_copy(g):
        part = half.at[pl.ds(core * count + 2 * g, 2)]
        return send(part, part, half_send, half_recv, pair)

    def pair_copy(t):
        part = coeffs_hbm.at[:, pl.ds(t * tile, tile)]
        return send(part, whole.at[core * count + t], pair_send, pair_recv, pair)

    lists = (
        (alpha_list_hbm, alpha_list),
        (alpha_kind_hbm, alpha_kind),
        (opp_list_hbm, opp_list),
        (opp_kind_hbm, opp_kind),
        (beta_list_hbm, beta_list),
        (beta_kind_hbm, beta_kind),
        (opp_beta_kind_hbm, opp_beta_kind),
    )
    load_coeffs = pltpu.make_async_copy(coeffs_hbm, coeffs, load_sem.at[0])
    load_lists = [pltpu.make_async_copy(src, dst, load_sem.at[2 + k]) for k, (src, dst) in enumerate(lists)]
    load_coeffs.start()
    for load in load_lists:
        load.start()
    for k, src in enumerate((beta_table_hbm, alpha_table_hbm, opp_alpha_table_hbm, opp_beta_table_hbm)):
        pltpu.make_async_copy(src, tables.at[k], load_sem.at[1]).start()

    barrier = pltpu.get_barrier_semaphore()
    for device in (chip(mates[LOW]), chip(mates[HIGH]), pair):
        pl.semaphore_signal(barrier, inc=1, device_id=device, device_id_type=pl.DeviceIdType.MESH)
    up, down = inside(z + 1), inside(z - 1)
    for there, offset in ((up, GROUP), (down, -GROUP)):

        @pl.when(there)
        def _():
            pl.semaphore_signal(
                barrier, inc=1, device_id=chip(me + offset), device_id_type=pl.DeviceIdType.MESH
            )

    for load in load_lists:
        load.wait()
    load_coeffs.wait()
    pltpu.make_async_copy(tables, tables, load_sem.at[1]).wait()

    pl.semaphore_wait(barrier, 3 + up.astype(jnp.int32) + down.astype(jnp.int32))

    for n in range(AHEAD):
        for link in (LOW, HIGH):
            own_copy(link, n, plans[link][n][1]).start()

    @pl.when(has_in[HIGH])
    def _():
        for c in range(summed, count):
            pass_copy(c).start()

    for t in range(count):
        pair_copy(t).start()
    for t in range(count):
        whole[core * count + t] = coeffs[:, t * tile : (t + 1) * tile]

    for r in range(3):

        @pl.when(jnp.logical_not(has_in[r]))
        def _():
            cross[r] = jnp.zeros_like(cross[r])

    @pl.when(corner & jnp.logical_not(has_in[LOW]))
    def _():
        sums[...] = jnp.zeros_like(sums)

    sources = [me, *mates] + [mates[r] - GROUP * steps[r] for r in range(3)]
    for slot, source in enumerate(sources):
        at = pl.ds(slot * tile, tile)
        tiles[:tile, at] = picked_tile(me, alpha_list, alpha_kind, alpha_table, source).astype(BF16)
        tiles[tile:, at] = picked_tile(me, opp_list, opp_kind, opp_alpha_table, source).astype(BF16)

    summing = corner & has_out[LOW]

    @pl.when(summing)
    def _():
        target = me + GROUP * steps[LOW]
        for slot, source in enumerate(mates):
            at = pl.ds(slot * tile, tile)
            onward[:tile, at] = picked_tile(target, alpha_list, alpha_kind, alpha_table, source).astype(BF16)
            onward[tile:, at] = picked_tile(target, opp_list, opp_kind, opp_alpha_table, source).astype(BF16)

    def product(weights, first, blocks):
        return jnp.dot(
            weights[:, first * tile : (first + len(blocks)) * tile],
            jnp.concatenate(blocks, axis=0),
            preferred_element_type=F32,
        )

    def wide_block(ref, r, g):
        return jnp.concatenate([ref[r, 2 * g], ref[r, 2 * g + 1]], axis=1)

    def beta_apply(data, kind, table, j):
        left, right = [], []
        for link in range(beta_list.shape[0]):
            left.append(data[beta_list[link, j]])
            right.append(table[kind[link, j]])
        return lax.dot_general(
            jnp.concatenate(left, axis=1),
            jnp.concatenate(right, axis=1),
            (((1,), (1,)), ((), ())),
            preferred_element_type=F32,
        )

    def same_spin(j):
        mine[:, columns(j)] = beta_apply(whole, beta_kind, beta_table, j)

    def in_plane(g):
        acc[:, wide(g)] = product(
            tiles, 0, [coeffs[:, wide(g)], *(wide_block(plane, r, g) for r in range(3))]
        )

    def cross_wait(first, g, there=True):
        @pl.when(has_in[first] & there)
        def _():
            if first == LOW or 2 * g >= summed:
                arrived(cross.at[LOW if first == LOW else DIAG, both(g)], cross_recv.at[first, g])
            else:
                arrived(cross.at[pl.ds(HIGH, 2), both(g)], cross_recv.at[first, g])

    def settle(g, added):
        total = added
        for t in range(2):
            half[core * count + 2 * g + t] = total[tile:, t * tile : (t + 1) * tile].astype(BF16)
        mine[:, wide(g)] += total[:tile]

    def close(g):
        there = True if 2 * g >= summed else middle
        cross_wait(LOW, g, there)
        cross_wait(HIGH, g, there)
        if 2 * g < summed:

            @pl.when(corner & has_in[LOW])
            def _():
                arrived(sums.at[both(g)], cross_recv.at[0, g])

        if 2 * g >= summed:
            settle(
                g,
                product(
                    tiles,
                    0,
                    [
                        coeffs[:, wide(g)],
                        *(wide_block(plane, r, g) for r in range(3)),
                        *(wide_block(cross, r, g) for r in range(3)),
                    ],
                ),
            )
        else:

            @pl.when(middle)
            def _():
                settle(g, acc[:, wide(g)] + product(tiles, 4, [wide_block(cross, r, g) for r in range(3)]))

            @pl.when(corner)
            def _():
                settle(g, acc[:, wide(g)] + jnp.concatenate([sums[2 * g], sums[2 * g + 1]], axis=1).astype(F32))

        half_copy(g).start()

    def sum_up(g):
        @pl.when(summing)
        def _():
            found = product(onward, 0, [wide_block(plane, r, g) for r in range(3)]).astype(BF16)
            for t in range(2):
                staged[2 * g + t] = found[:, t * tile : (t + 1) * tile]
                sum_copy(2 * g + t).start()

    seen = set()

    def take(link, n):
        kind, c = plans[link][n]
        if kind == "o":
            own_copy(link, n, c).wait_recv()
            if link == LOW:
                there = has_out[LOW] if c >= summed else has_out[LOW] & middle
            else:
                there = has_out[HIGH] & middle
            if link == LOW or c < summed:

                @pl.when(there)
                def _():
                    z_copy(link, c).start()

        elif kind == "r":
            relay_copy(link, n, c).wait_recv()

            @pl.when(middle & has_out[DIAG])
            def _():
                z_copy(DIAG, c).start()

            seen.add(c)
            if c < summed and c ^ 1 in seen:
                sum_up(c // 2)
                in_plane(c // 2)
        elif kind == "f":

            @pl.when(has_in[HIGH])
            def _():
                forward_copy(n, c).wait_recv()

    def issue(link, n):
        kind, c = plans[link][n]
        if kind == "o":
            own_copy(link, n, c).start()
        elif kind == "r":
            relay_copy(link, n, c).start()
        elif kind == "f":

            @pl.when(has_out[HIGH])
            def _():
                if c % 2 == 0:
                    k = c - summed
                    arrived(passing.at[pl.ds(k, 2)], pass_recv.at[k // 2])
                forward_copy(n, c).start()

        elif kind == "h":

            @pl.when(middle & has_in[HIGH])
            def _():
                hop_copy(c).start()

    last = len(plans[LOW])
    after = {i: [] for i in range(-1, last)}

    def put(i, what, *args):
        after[i].append((what, args))

    for j in range(count):
        put(-1, same_spin, j)
    for n, g in closing(plans, summed, relayed):
        put(n, close, g)

    arrived(whole.at[pl.ds((1 - core) * count, count)], pair_recv)
    for i in range(-1, last):
        if i >= 0:
            for link in (LOW, HIGH):
                take(link, i)
            if i + AHEAD < last:
                for link in (LOW, HIGH):
                    issue(link, i + AHEAD)
        for what, args in after[i]:
            what(*args)

    arrived(half.at[pl.ds((1 - core) * count, count)], half_recv)
    for j in range(count):
        mixed = beta_apply(half, opp_beta_kind, opp_beta_table, j)
        out[:, columns(j)] = (mine[:, columns(j)] + mixed).astype(BF16)

    sent(coeffs, own_send.at[LOW])
    sent(coeffs, own_send.at[HIGH])
    sent(whole.at[pl.ds(0, count)], pair_send)
    sent(half.at[pl.ds(0, count)], half_send)
    sent(plane.at[DIAG], relay_send)

    @pl.when(has_in[HIGH])
    def _():
        sent(passing, pass_send)

    @pl.when(has_out[HIGH])
    def _():
        sent(passing, forward_send)

    @pl.when(middle & has_in[HIGH])
    def _():
        sent(passing, hop_send)

    @pl.when(middle & has_out[LOW])
    def _():
        sent(plane.at[LOW], z_send.at[LOW])

    @pl.when(middle & has_out[HIGH])
    def _():
        sent(plane.at[HIGH, pl.ds(0, summed)], z_send.at[HIGH])
        sent(plane.at[DIAG], z_send.at[DIAG])

    @pl.when(summing)
    def _():
        sent(plane.at[LOW, pl.ds(0, relayed)], z_send.at[LOW])
        sent(staged, sum_send)


def local(group_count, coeffs, *rest):
    lists, tables = rest[:7], rest[7:]
    flat = coeffs.reshape(coeffs.shape[1:])
    rows, cols = flat.shape
    kinds, tile = tables[0].shape[:2]
    count = cols // tile
    relayed, groups = count // 2, count // 2
    summed = count - relayed
    operands = tuple(
        pltpu.with_memory_space_constraint(one, pltpu.HBM) for one in (*(one.T for one in lists), flat, *tables)
    )
    in_lists = [pltpu.SMEM(one.shape, one.dtype) for one in operands[:7]]
    dma = pltpu.SemaphoreType.DMA
    result = pl.pallas_call(
        functools.partial(kernel, group_count),
        out_shape=jax.ShapeDtypeStruct((rows, cols), BF16),
        in_specs=[pl.BlockSpec(memory_space=pltpu.HBM)] * len(operands),
        out_specs=pl.BlockSpec(memory_space=pltpu.VMEM),
        scratch_shapes=[
            *in_lists,
            pltpu.VMEM((rows, cols), BF16),
            pltpu.VMEM((len(tables), *tables[0].shape), BF16),
            pltpu.VMEM((3, count, rows, tile), BF16),
            pltpu.VMEM((3, count, rows, tile), BF16),
            pltpu.VMEM((summed, 2 * rows, tile), BF16),
            pltpu.VMEM((summed, 2 * rows, tile), BF16),
            pltpu.VMEM((relayed, rows, tile), BF16),
            pltpu.VMEM((2 * count, rows, tile), BF16),
            pltpu.VMEM((2 * count, rows, tile), BF16),
            pltpu.VMEM((2 * tile, cols), F32),
            pltpu.VMEM((rows, cols), F32),
            pltpu.VMEM((2 * tile, 7 * tile), BF16),
            pltpu.VMEM((2 * tile, 3 * tile), BF16),
            dma((9,)),
            dma((2,)),
            dma((2, slots_of(make_plans(summed, relayed))[1])),
            dma,
            dma((3,)),
            dma((2, groups)),
            dma,
            dma,
            dma((relayed // 2,)),
            dma,
            dma,
            dma,
            dma,
            dma,
            dma,
        ],
        compiler_params=pltpu.CompilerParams(
            collective_id=0, has_side_effects=True, vmem_limit_bytes=20000 * 1024
        ),
    )(*operands)
    return result.reshape(coeffs.shape)


def solution(mesh):
    halves = P("beta", None)
    return jax.shard_map(
        functools.partial(local, mesh.shape["alpha"] // GROUP),
        mesh=mesh,
        in_specs=(P(None, "alpha", "beta"), halves, halves, halves) + (P(),) * 8,
        out_specs=P(None, "alpha", "beta"),
        check_vma=False,
    )
```

profile of v0, /device:TPU:25, one launch (start us, length us, event | category | flops | bytes accessed | tf_op | source)
XLA Modules:
  0.0 31.9 jit_solution(2551569924628120027)
XLA Ops:
  0.0 31.1 %shard_map.118 = bf16[128,2048]{1,0:T(8,128)(2,1)S(1)} custom-call(s32[8,16]{1,0:T(8,128)} %bitcast.11, s32[8,16]{1,0:T(8,128)} %bitcast.12, s32[8,16]{1,0:T(8,128)} %bitcast.13, s32[4,16]{1,0:T(4,128)} %bitcast.14, s32[4,16]{1,0:T(4,128)} %bitcast.15, s32[3,16]{1,0:T(4,128)} %bitcast.16, s32[3,16]{1,0:T(4,128)} %bitcast.17, bf16[128,2048]{1,0:T(8,128)(2,1)} %bitcast.10, ...), custom_call_target="tpu_custom_call" | custom-call | tf_op jit(solution)/shard_map/pallas_call | solution.py:552
  31.1 0.8 %copy.14 = bf16[1,128,2048]{2,1,0:T(8,128)(2,1)} copy(bf16[1,128,2048]{2,1,0:T(8,128)(2,1)S(1)} %bitcast.9) | data formatting | bytes 1048576
where the time goes:
time: 32.1 us; the launch traced here: 31.9 us
  Pallas kernels  31.1 us (97%)
  local copies, waits for them, and re-layouts  0.8 us (2%)
    pallas_call x1, Pallas kernels, local(): pl.pallas_call(functools.partial(kernel, group_count), out_shape=jax.Shap...  31.1 us
    unnamed x1, local copies, waits for them, and re-layouts  0.8 us

commit v1 on v0

--- a/solution.py
+++ b/solution.py
@@ -9,9 +9,9 @@
 
 GROUP = 4
 AHEAD = 6
-FORWARD, STRIDE = 12, 10
+FORWARD, STRIDE = 15, 7
 DELAY = 3
-SHIFT = 1.5
+SHIFT = 3
 BF16, F32 = jnp.bfloat16, jnp.float32
 LOW, HIGH, DIAG = range(3)
 
@@ -288,11 +288,7 @@
                 barrier, inc=1, device_id=chip(me + offset), device_id_type=pl.DeviceIdType.MESH
             )
 
-    for load in load_lists:
-        load.wait()
     load_coeffs.wait()
-    pltpu.make_async_copy(tables, tables, load_sem.at[1]).wait()
-
     pl.semaphore_wait(barrier, 3 + up.astype(jnp.int32) + down.astype(jnp.int32))
 
     for n in range(AHEAD):
@@ -306,6 +302,10 @@
 
     for t in range(count):
         pair_copy(t).start()
+    for load in load_lists:
+        load.wait()
+    pltpu.make_async_copy(tables, tables, load_sem.at[1]).wait()
+
     for t in range(count):
         whole[core * count + t] = coeffs[:, t * tile : (t + 1) * tile]
 

time: 32.1 us -> 31.2 us (0.972)
  Pallas kernels: 31.1 us -> 30.1 us
    pallas_call x1, Pallas kernels: 31.1 us -> 30.1 us  [local(): pl.pallas_call(functools.partial(kernel, group_count), out_shape=jax.Shap...]
where the time goes in v1:
time: 31.2 us; the launch traced here: 30.9 us
  Pallas kernels  30.1 us (96%)
  local copies, waits for them, and re-layouts  0.8 us (3%)
    pallas_call x1, Pallas kernels, local(): pl.pallas_call(functools.partial(kernel, group_count), out_shape=jax.Shap...  30.1 us
    unnamed x1, local copies, waits for them, and re-layouts  0.8 us

profile of v1, /device:TPU:25, one launch (start us, length us, event | category | flops | bytes accessed | tf_op | source)
XLA Modules:
  0.0 30.9 jit_solution(17004355284462020236)
XLA Ops:
  0.0 30.1 %shard_map.118 = bf16[128,2048]{1,0:T(8,128)(2,1)S(1)} custom-call(s32[8,16]{1,0:T(8,128)} %bitcast.11, s32[8,16]{1,0:T(8,128)} %bitcast.12, s32[8,16]{1,0:T(8,128)} %bitcast.13, s32[4,16]{1,0:T(4,128)} %bitcast.14, s32[4,16]{1,0:T(4,128)} %bitcast.15, s32[3,16]{1,0:T(4,128)} %bitcast.16, s32[3,16]{1,0:T(4,128)} %bitcast.17, bf16[128,2048]{1,0:T(8,128)(2,1)} %bitcast.10, ...), custom_call_target="tpu_custom_call" | custom-call | tf_op jit(solution)/shard_map/pallas_call | solution.py:552
  30.1 0.8 %copy.14 = bf16[1,128,2048]{2,1,0:T(8,128)(2,1)} copy(bf16[1,128,2048]{2,1,0:T(8,128)(2,1)S(1)} %bitcast.9) | data formatting | bytes 1048576

commit v2 on v1

--- a/solution.py
+++ b/solution.py
@@ -12,6 +12,7 @@
 FORWARD, STRIDE = 15, 7
 DELAY = 3
 SHIFT = 3
+OPEN = (7, 5)
 BF16, F32 = jnp.bfloat16, jnp.float32
 LOW, HIGH, DIAG = range(3)
 
@@ -66,13 +67,32 @@
     return plans
 
 
+def issue_times(plans):
+    times = []
+    for most in OPEN:
+        per_link = ([], [])
+        for link, plan in enumerate(plans):
+            for n, (kind, c) in enumerate(plan):
+                need = {"r": ("o", c), "h": ("f", c)}.get(kind)
+                after = found_on(plans, 1 - link, need) if need else -1
+                per_link[link].append(max([n - most, after, -1, *per_link[link][-1:]]))
+        times.append(per_link)
+    return times
+
+
+def found_on(plans, link, item):
+    return plans[link].index(item)
+
+
 def slots_of(plans):
-    slots, most = ([], []), 0
+    times, slots, most = issue_times(plans), ([], []), 0
     for link, plan in enumerate(plans):
         held = []
         for n, (kind, _) in enumerate(plan):
-            sure = [k for k in range(n - AHEAD + 1) if plan[k][0] in ("o", "r")]
-            free = sure[-1] - AHEAD if sure else -1
+            free = len(plan)
+            for when in times:
+                sure = [k for k in range(when[link][n] + 1) if plan[k][0] in ("o", "r")]
+                free = min(free, when[link][sure[-1]] if sure else -1)
             if kind in ("o", "r", "f"):
                 spot = next((k for k, user in enumerate(held) if user <= free), len(held))
                 held[spot : spot + 1] = [n]
@@ -291,9 +311,44 @@
     load_coeffs.wait()
     pl.semaphore_wait(barrier, 3 + up.astype(jnp.int32) + down.astype(jnp.int32))
 
-    for n in range(AHEAD):
-        for link in (LOW, HIGH):
-            own_copy(link, n, plans[link][n][1]).start()
+    def issue(link, n):
+        kind, c = plans[link][n]
+        if kind == "o":
+            own_copy(link, n, c).start()
+        elif kind == "r":
+            relay_copy(link, n, c).start()
+        elif kind == "f":
+
+            @pl.when(has_out[HIGH])
+            def _():
+                if c % 2 == 0:
+                    k = c - summed
+                    arrived(passing.at[pl.ds(k, 2)], pass_recv.at[k // 2])
+                forward_copy(n, c).start()
+
+        elif kind == "h":
+
+            @pl.when(middle & has_in[HIGH])
+            def _():
+                hop_copy(c).start()
+
+    times = issue_times(plans)
+
+    def issue_after(i):
+        due = [[(link, n) for n in range(last) for link in (LOW, HIGH) if when[link][n] == i] for when in times]
+        if due[0] == due[1]:
+            for link, n in due[0]:
+                issue(link, n)
+        else:
+            for which in range(2):
+
+                @pl.when(core == which)
+                def _():
+                    for link, n in due[which]:
+                        issue(link, n)
+
+    last = len(plans[LOW])
+    issue_after(-1)
 
     @pl.when(has_in[HIGH])
     def _():
@@ -319,7 +374,7 @@
     def _():
         sums[...] = jnp.zeros_like(sums)
 
-    sources = [me, *mates] + [mates[r] - GROUP * steps[r] for r in range(3)]
+    sources = [me, mates[LOW], mates[DIAG], mates[HIGH]] + [mates[r] - GROUP * steps[r] for r in range(3)]
     for slot, source in enumerate(sources):
         at = pl.ds(slot * tile, tile)
         tiles[:tile, at] = picked_tile(me, alpha_list, alpha_kind, alpha_table, source).astype(BF16)
@@ -361,9 +416,10 @@
         mine[:, columns(j)] = beta_apply(whole, beta_kind, beta_table, j)
 
     def in_plane(g):
-        acc[:, wide(g)] = product(
-            tiles, 0, [coeffs[:, wide(g)], *(wide_block(plane, r, g) for r in range(3))]
-        )
+        blocks = [coeffs[:, wide(g)], wide_block(plane, LOW, g), wide_block(plane, DIAG, g)]
+        if 2 * g < summed:
+            blocks.append(wide_block(plane, HIGH, g))
+        acc[:, wide(g)] = product(tiles, 0, blocks)
 
     def cross_wait(first, g, there=True):
         @pl.when(has_in[first] & there)
@@ -390,18 +446,8 @@
                 arrived(sums.at[both(g)], cross_recv.at[0, g])
 
         if 2 * g >= summed:
-            settle(
-                g,
-                product(
-                    tiles,
-                    0,
-                    [
-                        coeffs[:, wide(g)],
-                        *(wide_block(plane, r, g) for r in range(3)),
-                        *(wide_block(cross, r, g) for r in range(3)),
-                    ],
-                ),
-            )
+            blocks = [wide_block(plane, HIGH, g), *(wide_block(cross, r, g) for r in range(3))]
+            settle(g, acc[:, wide(g)] + product(tiles, 3, blocks))
         else:
 
             @pl.when(middle)
@@ -446,8 +492,9 @@
                 z_copy(DIAG, c).start()
 
             seen.add(c)
-            if c < summed and c ^ 1 in seen:
-                sum_up(c // 2)
+            if c ^ 1 in seen:
+                if c < summed:
+                    sum_up(c // 2)
                 in_plane(c // 2)
         elif kind == "f":
 
@@ -455,28 +502,6 @@
             def _():
                 forward_copy(n, c).wait_recv()
 
-    def issue(link, n):
-        kind, c = plans[link][n]
-        if kind == "o":
-            own_copy(link, n, c).start()
-        elif kind == "r":
-            relay_copy(link, n, c).start()
-        elif kind == "f":
-
-            @pl.when(has_out[HIGH])
-            def _():
-                if c % 2 == 0:
-                    k = c - summed
-                    arrived(passing.at[pl.ds(k, 2)], pass_recv.at[k // 2])
-                forward_copy(n, c).start()
-
-        elif kind == "h":
-
-            @pl.when(middle & has_in[HIGH])
-            def _():
-                hop_copy(c).start()
-
-    last = len(plans[LOW])
     after = {i: [] for i in range(-1, last)}
 
     def put(i, what, *args):
@@ -492,9 +517,7 @@
         if i >= 0:
             for link in (LOW, HIGH):
                 take(link, i)
-            if i + AHEAD < last:
-                for link in (LOW, HIGH):
-                    issue(link, i + AHEAD)
+            issue_after(i)
         for what, args in after[i]:
             what(*args)
 

time: 31.2 us -> 30.7 us (0.984)
  Pallas kernels: 30.1 us -> 29.6 us
    pallas_call x1, Pallas kernels: 30.1 us -> 29.6 us  [local(): pl.pallas_call(functools.partial(kernel, group_count), out_shape=jax.Shap...]
where the time goes in v2:
time: 30.7 us; the launch traced here: 30.4 us
  Pallas kernels  29.6 us (96%)
  local copies, waits for them, and re-layouts  0.8 us (3%)
    pallas_call x1, Pallas kernels, local(): pl.pallas_call(functools.partial(kernel, group_count), out_shape=jax.Shap...  29.6 us
    unnamed x1, local copies, waits for them, and re-layouts  0.8 us

profile of v2, /device:TPU:25, one launch (start us, length us, event | category | flops | bytes accessed | tf_op | source)
XLA Modules:
  0.0 30.4 jit_solution(15600048208371779819)
XLA Ops:
  0.0 29.6 %shard_map.118 = bf16[128,2048]{1,0:T(8,128)(2,1)S(1)} custom-call(s32[8,16]{1,0:T(8,128)} %bitcast.11, s32[8,16]{1,0:T(8,128)} %bitcast.12, s32[8,16]{1,0:T(8,128)} %bitcast.13, s32[4,16]{1,0:T(4,128)} %bitcast.14, s32[4,16]{1,0:T(4,128)} %bitcast.15, s32[3,16]{1,0:T(4,128)} %bitcast.16, s32[3,16]{1,0:T(4,128)} %bitcast.17, bf16[128,2048]{1,0:T(8,128)(2,1)} %bitcast.10, ...), custom_call_target="tpu_custom_call" | custom-call | tf_op jit(solution)/shard_map/pallas_call | solution.py:575
  29.6 0.8 %copy.14 = bf16[1,128,2048]{2,1,0:T(8,128)(2,1)} copy(bf16[1,128,2048]{2,1,0:T(8,128)(2,1)S(1)} %bitcast.9) | data formatting | bytes 1048576

commit v3 on v2

--- a/solution.py
+++ b/solution.py
@@ -10,7 +10,7 @@
 GROUP = 4
 AHEAD = 6
 FORWARD, STRIDE = 15, 7
-DELAY = 3
+DELAY = 4
 SHIFT = 3
 OPEN = (7, 5)
 BF16, F32 = jnp.bfloat16, jnp.float32
@@ -155,9 +155,8 @@
     tiles,
     onward,
     load_sem,
-    own_send,
+    plane_send,
     plane_recv,
-    relay_send,
     z_send,
     cross_recv,
     sum_send,
@@ -227,7 +226,7 @@
         return send(
             coeffs.at[:, columns(c)],
             plane.at[to, c],
-            own_send.at[to],
+            plane_send,
             plane_recv.at[to, slots[to][n]],
             chip(mates[to]),
         )
@@ -236,7 +235,7 @@
         return send(
             plane.at[HIGH if to == LOW else LOW, c],
             plane.at[DIAG, c],
-            relay_send,
+            plane_send,
             plane_recv.at[to, slots[to][n]],
             chip(mates[to]),
         )
@@ -256,7 +255,7 @@
     def pass_copy(c):
         k = c - summed
         return send(
-            coeffs.at[:, columns(c)], passing.at[k], pass_send, pass_recv.at[k // 2], chip(me - GROUP * steps[HIGH])
+            coeffs.at[:, columns(c)], passing.at[k], pass_send, pass_recv, chip(me - GROUP * steps[HIGH])
         )
 
     def forward_copy(n, c):
@@ -321,9 +320,8 @@
 
             @pl.when(has_out[HIGH])
             def _():
-                if c % 2 == 0:
-                    k = c - summed
-                    arrived(passing.at[pl.ds(k, 2)], pass_recv.at[k // 2])
+                if c == summed:
+                    arrived(passing, pass_recv)
                 forward_copy(n, c).start()
 
         elif kind == "h":
@@ -526,11 +524,9 @@
         mixed = beta_apply(half, opp_beta_kind, opp_beta_table, j)
         out[:, columns(j)] = (mine[:, columns(j)] + mixed).astype(BF16)
 
-    sent(coeffs, own_send.at[LOW])
-    sent(coeffs, own_send.at[HIGH])
+    sent(plane, plane_send)
     sent(whole.at[pl.ds(0, count)], pair_send)
     sent(half.at[pl.ds(0, count)], half_send)
-    sent(plane.at[DIAG], relay_send)
 
     @pl.when(has_in[HIGH])
     def _():
@@ -593,14 +589,13 @@
             pltpu.VMEM((2 * tile, 7 * tile), BF16),
             pltpu.VMEM((2 * tile, 3 * tile), BF16),
             dma((9,)),
-            dma((2,)),
+            dma,
             dma((2, slots_of(make_plans(summed, relayed))[1])),
-            dma,
             dma((3,)),
             dma((2, groups)),
             dma,
             dma,
-            dma((relayed // 2,)),
+            dma,
             dma,
             dma,
             dma,

time: 30.7 us -> 30.6 us (level)
  no operation moved by 1% of the time
where the time goes in v3:
time: 30.6 us; the launch traced here: 30.3 us
  Pallas kernels  29.5 us (96%)
  local copies, waits for them, and re-layouts  0.8 us (3%)
    pallas_call x1, Pallas kernels, local(): pl.pallas_call(functools.partial(kernel, group_count), out_shape=jax.Shap...  29.5 us
    unnamed x1, local copies, waits for them, and re-layouts  0.8 us

profile of v3, /device:TPU:25, one launch (start us, length us, event | category | flops | bytes accessed | tf_op | source)
XLA Modules:
  0.0 30.3 jit_solution(13082238782994389099)
XLA Ops:
  0.0 29.5 %shard_map.118 = bf16[128,2048]{1,0:T(8,128)(2,1)S(1)} custom-call(s32[8,16]{1,0:T(8,128)} %bitcast.11, s32[8,16]{1,0:T(8,128)} %bitcast.12, s32[8,16]{1,0:T(8,128)} %bitcast.13, s32[4,16]{1,0:T(4,128)} %bitcast.14, s32[4,16]{1,0:T(4,128)} %bitcast.15, s32[3,16]{1,0:T(4,128)} %bitcast.16, s32[3,16]{1,0:T(4,128)} %bitcast.17, bf16[128,2048]{1,0:T(8,128)(2,1)} %bitcast.10, ...), custom_call_target="tpu_custom_call" | custom-call | tf_op jit(solution)/shard_map/pallas_call | solution.py:571
  29.5 0.8 %copy.14 = bf16[1,128,2048]{2,1,0:T(8,128)(2,1)} copy(bf16[1,128,2048]{2,1,0:T(8,128)(2,1)S(1)} %bitcast.9) | data formatting | bytes 1048576
